TPU v7x, 512 devices: a whole 4x4x16 slice. The times are simulated.
512 devices in a mesh: dp: 16 (over z), expert: 32 (over x, y, core).
Axes of the slice: x: 4, y: 4, z: 16, core: 2. Of those that a mesh axis runs over, the one named last changes fastest.
Arguments:
- tokens: bfloat16 [4096, 4096], P('expert', 'dp'), may hold values from -6 to 6
- route_ids: int32 [4096, 8], P('expert'), may hold values from 0 to 31, all different within a row; in each aligned block of 128 rows (0 to 127, 128 to 255, ...) at most 40 rows name the same one
- route_weights: bfloat16 [4096, 8], P('expert'), may hold values from 0.099609375 to 0.3984375
- gate_weight: bfloat16 [32, 4096, 768], P('expert', 'dp'), may hold values from -0.09375 to 0.09375
- up_weight: bfloat16 [32, 4096, 768], P('expert', 'dp'), may hold values from -0.09375 to 0.09375
- down_weight: bfloat16 [32, 768, 4096], P('expert', None, 'dp'), may hold values from -0.21875 to 0.21875
- out_grad: bfloat16 [4096, 4096], P('expert', 'dp'), may hold values from -3 to 3
Outputs:
- mixed: bfloat16 [4096, 4096], P('expert', 'dp')
- input_grad: bfloat16 [4096, 4096], P('expert', 'dp')
- gate_weight_grad: float32 [32, 4096, 768], P('expert', 'dp')
- up_weight_grad: float32 [32, 4096, 768], P('expert', 'dp')
- down_weight_grad: float32 [32, 768, 4096], P('expert', None, 'dp')
Inputs may be any that keep to these rules, and one draw needn't show every extreme that they name: `route_ids`: each row names 8 different experts. In each aligned block of 128 rows (the tokens of one index of expert) no expert is named by more than 40 rows, a bound that some block reaches.
All inputs are finite; a program needn't handle non-finite values.
Results may differ from a plain program's by a relative error of at most 0.039.
Values may be sent and summed in bfloat16 or wider, within the bound.
A program may use at most 64 MiB of HBM per device.

v0:
```python
import jax
import jax.numpy as jnp
from jax import lax
from jax.sharding import PartitionSpec as P


def contract_rows(first_op, second_op):
    return lax.dot_general(
        first_op, second_op, (((0,), (0,)), ((), ())), preferred_element_type=jnp.float32
    )


def contract_cols(first_op, second_op):
    return lax.dot_general(
        first_op, second_op, (((1,), (1,)), ((), ())), preferred_element_type=jnp.float32
    )


def expert_forward(expert_rows, weight_g, weight_u, weight_d):
    partial_gate = jnp.dot(expert_rows, weight_g, preferred_element_type=jnp.float32)
    partial_up = jnp.dot(expert_rows, weight_u, preferred_element_type=jnp.float32)
    gate_pre, up_pre = (
        lax.psum(partial_gate.astype(jnp.bfloat16), "dp").astype(jnp.float32),
        lax.psum(partial_up.astype(jnp.bfloat16), "dp").astype(jnp.float32),
    )
    hidden = (jax.nn.silu(gate_pre) * up_pre).astype(jnp.bfloat16)
    produced = jnp.dot(hidden, weight_d, preferred_element_type=jnp.float32).astype(jnp.bfloat16)
    return (gate_pre, up_pre, hidden, produced)


def expert_backward(expert_rows, upstream, gate_pre, up_pre, hidden, weight_g, weight_u, weight_d):
    partial_value = contract_cols(upstream, weight_d)
    hidden_grad = lax.psum(partial_value.astype(jnp.bfloat16), "dp").astype(jnp.float32)
    sigmoid_gate = jax.nn.sigmoid(gate_pre)
    gate_delta = (
        hidden_grad * up_pre * sigmoid_gate * (1.0 + gate_pre * (1.0 - sigmoid_gate))
    ).astype(jnp.bfloat16)
    up_delta = (hidden_grad * jax.nn.silu(gate_pre)).astype(jnp.bfloat16)
    down_grad = contract_rows(hidden, upstream)
    gate_grad = contract_rows(expert_rows, gate_delta)
    up_grad = contract_rows(expert_rows, up_delta)
    back_rows = (contract_cols(gate_delta, weight_g) + contract_cols(up_delta, weight_u)).astype(
        jnp.bfloat16
    )
    return (gate_grad, up_grad, down_grad, back_rows)


def shards(tokens, route_ids, route_weights, gate_weight, up_weight, down_weight, out_grad):
    expert_count = lax.axis_size("expert")
    tok_count = tokens.shape[0]
    width = tokens.shape[1]
    top_count = route_ids.shape[1]
    capacity = min(tok_count, tok_count * top_count // expert_count + tok_count // 16)
    row_total = expert_count * capacity
    weight_g = gate_weight[0]
    weight_u = up_weight[0]
    weight_d = down_weight[0]
    every_tok, every_grad, every_weight = (
        lax.all_gather(tokens, "expert", axis=0, tiled=True),
        lax.all_gather(out_grad, "expert", axis=0, tiled=True),
        lax.all_gather(route_weights, "expert", axis=0, tiled=True),
    )
    every_ids = lax.all_gather(route_ids, "expert", axis=0, tiled=True)
    my_expert = lax.axis_index("expert")
    chosen = every_ids == my_expert
    hit_count = jnp.sum(chosen.astype(jnp.int32), axis=1).reshape(expert_count, tok_count)
    hit_rank = jnp.cumsum(hit_count, axis=1) - hit_count
    block_start = (jnp.arange(expert_count, dtype=jnp.int32) * capacity)[:, None]
    dest_row = jnp.where(hit_count > 0, block_start + hit_rank, row_total).reshape(-1)
    tok_weight = jnp.sum(jnp.where(chosen, every_weight.astype(jnp.float32), 0.0), axis=1)
    expert_rows = (
        jnp.zeros((row_total, width), jnp.bfloat16).at[dest_row].set(every_tok, mode="drop")
    )
    row_weight = jnp.zeros((row_total,), jnp.float32).at[dest_row].set(tok_weight, mode="drop")
    gate_pre, up_pre, hidden, produced = expert_forward(expert_rows, weight_g, weight_u, weight_d)
    safe_row = jnp.minimum(dest_row, row_total - 1)
    present = (hit_count.reshape(-1) > 0).astype(jnp.float32)[:, None]
    weighted = (
        (row_weight[:, None] * produced.astype(jnp.float32))
        .astype(jnp.bfloat16)
        .astype(jnp.float32)
    )
    mixed = lax.psum_scatter(
        (weighted[safe_row] * present).astype(jnp.bfloat16),
        "expert",
        scatter_dimension=0,
        tiled=True,
    )
    grad_rows = (
        jnp.zeros((row_total, width), jnp.bfloat16).at[dest_row].set(every_grad, mode="drop")
    )
    upstream = (row_weight[:, None] * grad_rows.astype(jnp.float32)).astype(jnp.bfloat16)
    gate_grad, up_grad, down_grad, back_rows = expert_backward(
        expert_rows, upstream, gate_pre, up_pre, hidden, weight_g, weight_u, weight_d
    )
    input_grad = lax.psum_scatter(
        (back_rows.astype(jnp.float32)[safe_row] * present).astype(jnp.bfloat16),
        "expert",
        scatter_dimension=0,
        tiled=True,
    )
    return (mixed, input_grad, gate_grad[None], up_grad[None], down_grad[None])


def solution(mesh):
    return jax.shard_map(
        shards,
        mesh=mesh,
        in_specs=(
            P("expert", "dp"),
            P("expert", None),
            P("expert", None),
            P("expert", "dp", None),
            P("expert", "dp", None),
            P("expert", None, "dp"),
            P("expert", "dp"),
        ),
        out_specs=(
            P("expert", "dp"),
            P("expert", "dp"),
            P("expert", "dp", None),
            P("expert", "dp", None),
            P("expert", None, "dp"),
        ),
        check_vma=False,
    )
```

profile of v0, /device:TPU:2, one launch (start us, length us, event | category | flops | bytes accessed | tf_op | source)
XLA Modules:
  0.0 580.4 jit_solution(8875477676704722195)
XLA Ops:
  8.0 0.7 all-gather.5.cloned.1.call-update
  8.7 27.1 %all_gather.13 = bf16[4096,8]{0,1:T(8,128)(2,1)S(1)} all-gather(bf16[128,8]{0,1:T(8,128)(2,1)} %param.9), channel_id=1, replica_groups=mesh['dp'=16,'expert'=32] {'expert'}, dimensions={0}, use_global_device_ids=true | all-gather | bytes 67584 | tf_op jit(solution)/shard_map/all_gather | solution.py:61
  35.8 22.3 %all_gather.12 = s32[4096,8]{0,1:T(8,128)S(1)} all-gather(s32[128,8]{0,1:T(8,128)} %param.8), channel_id=1, replica_groups=mesh['dp'=16,'expert'=32] {'expert'}, dimensions={0}, use_global_device_ids=true | all-gather | bytes 135168 | tf_op jit(solution)/shard_map/all_gather | solution.py:63
  58.7 15.5 %scatter_custom_fusion = f32[1280]{0:T(1024)S(1)} fusion(s32[4096]{0:T(1024)S(1)} %bitcast.45, f32[4096]{0:T(1024)S(1)} %get-tuple-element.10, f32[]{:T(128)} %constant.8.clone.1), kind=kCustom, calls=%fused_computation.56 | custom fusion | bytes 5124 | tf_op jit(solution)/shard_map/scatter | solution.py:74
  74.2 18.3 %scatter_custom_fusion.1 = bf16[1280,256]{1,0:T(8,128)(2,1)S(1)} fusion(s32[4096]{0:T(1024)S(1)} %bitcast.46, bf16[4096,256]{1,0:T(8,128)(2,1)} %all-gather.3.cloned.1.call-done, bf16[]{:T(256)} %constant.13.clone.1), kind=kCustom, calls=%fused_computation.46 | custom fusion | bytes 655872 | tf_op jit(solution)/shard_map/scatter | solution.py:72
  92.5 3.2 convolution_convert_fusion.1
  95.7 2.0 convolution_convert_fusion.2
  97.7 38.0 %all-gather.5.cloned.1.call-done = bf16[4096,256]{1,0:T(8,128)(2,1)} async-done(((bf16[128,256]{1,0:T(8,128)(2,1)}), bf16[4096,256]{1,0:T(8,128)(2,1)}) %all-gather.5.cloned.1.call-update) | async-done | bytes 2097168 | tf_op jit(solution)/shard_map/all_gather | solution.py:60
  135.7 18.3 %scatter_custom_fusion.2 = bf16[1280,256]{1,0:T(8,128)(2,1)S(1)} fusion(s32[4096]{0:T(1024)S(1)} %bitcast.47, bf16[4096,256]{1,0:T(8,128)(2,1)} %all-gather.5.cloned.1.call-done, bf16[]{:T(256)} %constant.13.clone.1), kind=kCustom, calls=%fused_computation.44 | custom fusion | bytes 655872 | tf_op jit(solution)/shard_map/scatter | solution.py:90
  154.0 2.0 convolution_convert_fusion
  156.3 167.8 %all-reduce.3.cloned.1.call-done = (bf16[1280,768]{1,0:T(8,128)(2,1)}, bf16[1280,768]{1,0:T(8,128)(2,1)}, bf16[1280,768]{1,0:T(8,128)(2,1)}) async-done(((bf16[1280,768]{1,0:T(8,128)(2,1)}, bf16[1280,768]{1,0:T(8,128)(2,1)}, bf16[1280,768]{1,0:T(8,128)(2,1)}), (bf16[1280,768]{1,0:T(8,128)(2,1)}, bf16[1280,768]{1,0:T(8,128)(2,1)}, bf16[1280,768]{1,0:T(8,128)(2,1)})) %all-reduce.3.cloned.1.call-update) | async-done | bytes 5898256 | tf_op jit(solution)/shard_map/psum | solution.py:24
  324.2 4.2 fusion.4
  328.4 0.7 fusion.12
  329.2 0.7 fusion.19
  330.9 0.7 fusion.14
  331.7 16.1 %gather_fusion.1 = f32[4096,256]{1,0:T(8,128)} fusion(f32[1280,256]{1,0:T(8,128)S(1)} %fusion.14, s32[4096]{0:T(1024)S(1)} %broadcast_clamp_fusion), kind=kCustom, calls=%fused_computation.1 | custom fusion | bytes 8404992 | tf_op jit(solution)/shard_map/gather | solution.py:97
  347.8 16.2 %gather_fusion = f32[4096,256]{1,0:T(8,128)} fusion(f32[1280,256]{1,0:T(8,128)S(1)} %fusion.12, s32[4096]{0:T(1024)S(1)} %broadcast_clamp_fusion), kind=kCustom, calls=%fused_computation | custom fusion | bytes 8404992 | tf_op jit(solution)/shard_map/gather | solution.py:84
  364.0 5.1 multiply_convert_fusion
  369.7 0.9 copy-done.4
  370.8 1.6 convolution_bitcast_fusion.1
  372.4 1.6 convolution_bitcast_fusion.2
  374.2 1.8 convolution_bitcast_fusion
  376.0 91.4 %reduce-scatter.5.cloned.1.call-done = bf16[128,256]{1,0:T(8,128)(2,1)} async-done(((bf16[4096,256]{1,0:T(8,128)(2,1)}), bf16[128,256]{1,0:T(8,128)(2,1)}) %reduce-scatter.5.cloned.1.call-update) | async-done | bytes 65552 | tf_op jit(solution)/shard_map/reduce_scatter | solution.py:96
  467.5 106.4 %reduce-scatter.3.cloned.1.call-done = bf16[128,256]{1,0:T(8,128)(2,1)} async-done(((bf16[4096,256]{1,0:T(8,128)(2,1)}), bf16[128,256]{1,0:T(8,128)(2,1)}) %reduce-scatter.3.cloned.1.call-update) | async-done | bytes 65552 | tf_op jit(solution)/shard_map/reduce_scatter | solution.py:83
  (44 shorter events, 3.6 us)
Async XLA Ops:
  7.2 146.9 %copy-start = (bf16[1,768,256]{2,1,0:T(8,128)(2,1)S(1)}, bf16[1,768,256]{2,1,0:T(8,128)(2,1)}, u32[]{:S(2)}) copy-start(bf16[1,768,256]{2,1,0:T(8,128)(2,1)} %param.12) | copy-start | bytes 1179652
  7.2 67.0 %all-gather.3.cloned.1.call-start = ((), (), s32[]{:S(2)}) async-start(), calls=%async_computation.2 | async-start | bytes 2162688 | tf_op jit(solution)/shard_map/all_gather | solution.py:59
  7.9 127.8 %all-gather.5.cloned.1.call-start = ((), (), s32[]{:S(2)}) async-start(), calls=%async_computation.4 | async-start | bytes 2162688 | tf_op jit(solution)/shard_map/all_gather | solution.py:60
  8.7 315.5 %all-reduce.3.cloned.1.call-start = ((), (), s32[]{:S(2)}) async-start(), calls=%async_computation.6 | async-start | bytes 11796480 | tf_op jit(solution)/shard_map/psum | solution.py:24
  58.2 37.6 %copy-start.11 = (bf16[1,256,768]{2,1,0:T(8,128)(2,1)S(1)}, bf16[1,256,768]{2,1,0:T(8,128)(2,1)}, u32[]{:S(2)}) copy-start(bf16[1,256,768]{2,1,0:T(8,128)(2,1)} %param.10) | copy-start | bytes 1179652
  92.5 5.2 copy-start.5
  154.0 2.0 copy-start.9
  156.1 311.4 %reduce-scatter.5.cloned.1.call-start = ((), (), s32[]{:S(2)}) async-start(), calls=%async_computation.5 | async-start | bytes 2162688 | tf_op jit(solution)/shard_map/reduce_scatter | solution.py:96
  328.4 1.5 copy-start.1
  328.4 1.9 copy-start.7
  328.4 2.5 copy-start.3
  329.1 1.8 copy-start.12
  369.1 1.5 copy-start.4
  369.1 1.7 copy-start.6
  369.1 204.7 %reduce-scatter.3.cloned.1.call-start = ((), (), s32[]{:S(2)}) async-start(), calls=%async_computation.3 | async-start | bytes 2162688 | tf_op jit(solution)/shard_map/reduce_scatter | solution.py:83
  370.8 1.6 copy-start.2
  372.4 1.6 copy-start.8
  372.4 1.8 copy-start.10
Sparse Core Ops, SparseCore 0:
  11.1 62.9 all-gather.2
  77.3 58.3 all-gather.4
  156.2 167.9 all-reduce.2
  369.3 98.1 reduce-scatter.4
  472.3 101.5 reduce-scatter.2
where the time goes:
time: 581 us; the launch traced here: 580 us
  waiting for transfers between devices  406 us (70%)
  local copies, waits for them, and re-layouts  86.8 us (15%)
  blocking collectives  49.4 us (9%)
  matrix products  14.3 us (2%)
  between operations  14 us (2%)
  other arithmetic  9.82 us (2%)
    psum x1, waiting for transfers between devices, expert_forward(): lax.psum(partial_up.astype(jnp.bfloat16), 'dp').astype(jnp.float32)  168 us
    reduce_scatter x1, waiting for transfers between devices, shards(): lax.psum_scatter((weighted[safe_row] * present).astype(jnp.bfloat16), 'ex...  106 us
    reduce_scatter x1, waiting for transfers between devices, shards(): lax.psum_scatter((back_rows.astype(jnp.float32)[safe_row] * present).asty...  91.4 us
    all_gather x1, waiting for transfers between devices, shards(): lax.all_gather(out_grad, 'expert', axis=0, tiled=True)  38 us
    scatter x2, local copies, waits for them, and re-layouts, shards(): jnp.zeros((row_total, width), jnp.bfloat16).at[dest_row]  36.6 us
    all_gather x1, blocking collectives, shards(): lax.all_gather(route_weights, 'expert', axis=0, tiled=True)  27.1 us
    all_gather x1, blocking collectives, shards(): every_ids = lax.all_gather(route_ids, 'expert', axis=0, tiled=True)  22.3 us
    gather x1, local copies, waits for them, and re-layouts, shards(): weighted[safe_row] * present  16.2 us
  transfers between devices with their start and end apart: 5, of which 4 were waited for; matrix products, arithmetic and copies ran while one was open for 8% of the time, Pallas kernels for 0%

commit v1 on v0

--- a/solution.py
+++ b/solution.py
@@ -2,6 +2,11 @@
 import jax.numpy as jnp
 from jax import lax
 from jax.sharding import PartitionSpec as P
+
+
+def gather_and_add(array, axis):
+    parts = lax.all_gather(array, axis)
+    return jnp.sum(parts, axis=0)
 
 
 def contract_rows(first_op, second_op):
@@ -21,7 +26,7 @@
     partial_up = jnp.dot(expert_rows, weight_u, preferred_element_type=jnp.float32)
     gate_pre, up_pre = (
         lax.psum(partial_gate.astype(jnp.bfloat16), "dp").astype(jnp.float32),
-        lax.psum(partial_up.astype(jnp.bfloat16), "dp").astype(jnp.float32),
+        gather_and_add(partial_up.astype(jnp.bfloat16), "dp").astype(jnp.float32),
     )
     hidden = (jax.nn.silu(gate_pre) * up_pre).astype(jnp.bfloat16)
     produced = jnp.dot(hidden, weight_d, preferred_element_type=jnp.float32).astype(jnp.bfloat16)

time: 581 us -> 887 us (1.53)
  waiting for transfers between devices: 406 us -> 701 us
  other arithmetic: 9.82 us -> 20.9 us
    all_gather x0 -> x1, waiting for transfers between devices: none -> 317 us  [gather_and_add(): parts = lax.all_gather(array, axis)]
    psum x1, waiting for transfers between devices: 168 us -> 145 us  [expert_forward(): lax.psum(partial_gate.astype(jnp.bfloat16), 'dp').astype(jnp.float32)]
    all_gather x1, waiting for transfers between devices: 0.02 us -> 15.5 us  [shards(): lax.all_gather(tokens, 'expert', axis=0, tiled=True)]
    all_gather x1, waiting for transfers between devices: 38 us -> 24.3 us  [shards(): lax.all_gather(out_grad, 'expert', axis=0, tiled=True)]
    reduce_sum x0 -> x1, other arithmetic: none -> 11.3 us  [gather_and_add(): return jnp.sum(parts, axis=0)]
  transfers between devices with their start and end apart: 5 -> 6, of which waited for: 4 -> 6; matrix products, arithmetic and copies ran while one was open for 8% -> 9% of each run, Pallas kernels for 0% -> 0%
where the time goes in v1:
time: 887 us
  waiting for transfers between devices  701 us (79%)
  local copies, waits for them, and re-layouts  86.7 us (10%)
  blocking collectives  49.4 us (6%)
  other arithmetic  20.9 us (2%)
  matrix products  14.3 us (2%)
  between operations  14.3 us (2%)
    all_gather x1, waiting for transfers between devices, gather_and_add(): parts = lax.all_gather(array, axis)  317 us
    psum x1, waiting for transfers between devices, expert_forward(): lax.psum(partial_gate.astype(jnp.bfloat16), 'dp').astype(jnp.float32)  145 us
    reduce_scatter x1, waiting for transfers between devices, shards(): lax.psum_scatter((weighted[safe_row] * present).astype(jnp.bfloat16), 'ex...  106 us
    reduce_scatter x1, waiting for transfers between devices, shards(): lax.psum_scatter((back_rows.astype(jnp.float32)[safe_row] * present).asty...  90.8 us
    scatter x2, local copies, waits for them, and re-layouts, shards(): jnp.zeros((row_total, width), jnp.bfloat16).at[dest_row]  36.6 us
    all_gather x1, blocking collectives, shards(): lax.all_gather(route_weights, 'expert', axis=0, tiled=True)  27.1 us
    all_gather x1, waiting for transfers between devices, shards(): lax.all_gather(out_grad, 'expert', axis=0, tiled=True)  24.3 us
    all_gather x1, blocking collectives, shards(): every_ids = lax.all_gather(route_ids, 'expert', axis=0, tiled=True)  22.3 us
  transfers between devices with their start and end apart: 6, of which 6 were waited for; matrix products, arithmetic and copies ran while one was open for 9% of the time, Pallas kernels for 0%

profile of v1, /device:TPU:2, one launch (start us, length us, event | category | flops | bytes accessed | tf_op | source)
XLA Modules:
  0.0 886.7 jit_solution(1524954169812980217)
XLA Ops:
  8.7 27.1 %all_gather.19 = bf16[4096,8]{0,1:T(8,128)(2,1)S(1)} all-gather(bf16[128,8]{0,1:T(8,128)(2,1)} %param.9), channel_id=1, replica_groups=mesh['dp'=16,'expert'=32] {'expert'}, dimensions={0}, use_global_device_ids=true | all-gather | bytes 67584 | tf_op jit(solution)/shard_map/all_gather | solution.py:66
  35.8 22.3 %all_gather.18 = s32[4096,8]{0,1:T(8,128)S(1)} all-gather(s32[128,8]{0,1:T(8,128)} %param.8), channel_id=1, replica_groups=mesh['dp'=16,'expert'=32] {'expert'}, dimensions={0}, use_global_device_ids=true | all-gather | bytes 135168 | tf_op jit(solution)/shard_map/all_gather | solution.py:68
  58.6 15.5 %all-gather.5.cloned.1.call-done = bf16[4096,256]{1,0:T(8,128)(2,1)} async-done(((bf16[128,256]{1,0:T(8,128)(2,1)}), bf16[4096,256]{1,0:T(8,128)(2,1)}) %all-gather.5.cloned.1.call-update) | async-done | bytes 2097168 | tf_op jit(solution)/shard_map/all_gather | solution.py:64
  74.2 18.3 %scatter_custom_fusion.1 = bf16[1280,256]{1,0:T(8,128)(2,1)S(1)} fusion(s32[4096]{0:T(1024)S(1)} %bitcast.47, bf16[4096,256]{1,0:T(8,128)(2,1)} %all-gather.5.cloned.1.call-done, bf16[]{:T(256)} %constant.13.clone.1), kind=kCustom, calls=%fused_computation.46 | custom fusion | bytes 655872 | tf_op jit(solution)/shard_map/scatter | solution.py:77
  92.5 3.2 convolution_convert_fusion.1
  95.7 15.5 %scatter_custom_fusion = f32[1280]{0:T(1024)S(1)} fusion(s32[4096]{0:T(1024)S(1)} %bitcast.48, f32[4096]{0:T(1024)S(1)} %get-tuple-element.9, f32[]{:T(128)} %constant.8.clone.1), kind=kCustom, calls=%fused_computation.56 | custom fusion | bytes 5124 | tf_op jit(solution)/shard_map/scatter | solution.py:79
  111.3 24.3 %all-gather.7.cloned.1.call-done = bf16[4096,256]{1,0:T(8,128)(2,1)} async-done(((bf16[128,256]{1,0:T(8,128)(2,1)}), bf16[4096,256]{1,0:T(8,128)(2,1)}) %all-gather.7.cloned.1.call-update) | async-done | bytes 2097168 | tf_op jit(solution)/shard_map/all_gather | solution.py:65
  135.6 18.3 %scatter_custom_fusion.2 = bf16[1280,256]{1,0:T(8,128)(2,1)S(1)} fusion(s32[4096]{0:T(1024)S(1)} %bitcast.49, bf16[4096,256]{1,0:T(8,128)(2,1)} %all-gather.7.cloned.1.call-done, bf16[]{:T(256)} %constant.13.clone.1), kind=kCustom, calls=%fused_computation.44 | custom fusion | bytes 655872 | tf_op jit(solution)/shard_map/scatter | solution.py:95
  153.9 1.9 convolution_convert_fusion.2
  155.8 2.0 convolution_convert_fusion
  158.1 316.9 %all-gather.9.cloned.1.call-done = bf16[20480,768]{1,0:T(8,128)(2,1)} async-done(((bf16[1280,768]{1,0:T(8,128)(2,1)}), bf16[20480,768]{1,0:T(8,128)(2,1)}) %all-gather.9.cloned.1.call-update) | async-done | bytes 31457296 | tf_op jit(solution)/shard_map/all_gather | solution.py:8
  475.1 11.3 %reduce_sum.35 = bf16[1280,768]{1,0:T(8,128)(2,1)S(1)} reduce(bf16[16,1280,768]{2,1,0:T(8,128)(2,1)} %bitcast.41, bf16[]{:T(256)} %constant.13.clone.1), dimensions={0}, to_apply=%region_6.7 | reduce | flops 14745600 | bytes 33423362 | tf_op jit(solution)/shard_map/reduce_sum | solution.py:9
  486.3 144.7 %all-reduce.3.cloned.1.call-done = (bf16[1280,768]{1,0:T(8,128)(2,1)}, bf16[1280,768]{1,0:T(8,128)(2,1)}) async-done(((bf16[1280,768]{1,0:T(8,128)(2,1)}, bf16[1280,768]{1,0:T(8,128)(2,1)}), (bf16[1280,768]{1,0:T(8,128)(2,1)}, bf16[1280,768]{1,0:T(8,128)(2,1)})) %all-reduce.3.cloned.1.call-update) | async-done | bytes 3932176 | tf_op jit(solution)/shard_map/psum | solution.py:28
  631.1 3.9 fusion.4
  637.7 0.7 fusion.14
  638.4 16.1 %gather_fusion.1 = f32[4096,256]{1,0:T(8,128)} fusion(f32[1280,256]{1,0:T(8,128)S(1)} %fusion.14, s32[4096]{0:T(1024)S(1)} %broadcast_clamp_fusion), kind=kCustom, calls=%fused_computation.1 | custom fusion | bytes 8404992 | tf_op jit(solution)/shard_map/gather | solution.py:102
  654.5 16.0 %gather_fusion = f32[4096,256]{1,0:T(8,128)} fusion(f32[1280,256]{1,0:T(8,128)S(1)} %fusion.12, s32[4096]{0:T(1024)S(1)} %broadcast_clamp_fusion), kind=kCustom, calls=%fused_computation | custom fusion | bytes 8404992 | tf_op jit(solution)/shard_map/gather | solution.py:89
  670.5 5.2 multiply_convert_fusion
  676.4 0.9 copy-done.5
  677.4 1.6 convolution_bitcast_fusion.1
  679.0 1.6 convolution_bitcast_fusion.2
  680.8 1.8 convolution_bitcast_fusion
  682.6 90.8 %reduce-scatter.5.cloned.1.call-done = bf16[128,256]{1,0:T(8,128)(2,1)} async-done(((bf16[4096,256]{1,0:T(8,128)(2,1)}), bf16[128,256]{1,0:T(8,128)(2,1)}) %reduce-scatter.5.cloned.1.call-update) | async-done | bytes 65552 | tf_op jit(solution)/shard_map/reduce_scatter | solution.py:101
  773.5 106.4 %reduce-scatter.3.cloned.1.call-done = bf16[128,256]{1,0:T(8,128)(2,1)} async-done(((bf16[4096,256]{1,0:T(8,128)(2,1)}), bf16[128,256]{1,0:T(8,128)(2,1)}) %reduce-scatter.3.cloned.1.call-update) | async-done | bytes 65552 | tf_op jit(solution)/shard_map/reduce_scatter | solution.py:88
  (50 shorter events, 5.8 us)
Async XLA Ops:
  7.2 148.7 %copy-start = (bf16[1,768,256]{2,1,0:T(8,128)(2,1)S(1)}, bf16[1,768,256]{2,1,0:T(8,128)(2,1)}, u32[]{:S(2)}) copy-start(bf16[1,768,256]{2,1,0:T(8,128)(2,1)} %param.12) | copy-start | bytes 1179652
  7.2 67.0 %all-gather.5.cloned.1.call-start = ((), (), s32[]{:S(2)}) async-start(), calls=%async_computation.2 | async-start | bytes 2162688 | tf_op jit(solution)/shard_map/all_gather | solution.py:64
  7.9 127.6 %all-gather.7.cloned.1.call-start = ((), (), s32[]{:S(2)}) async-start(), calls=%async_computation.4 | async-start | bytes 2162688 | tf_op jit(solution)/shard_map/all_gather | solution.py:65
  8.7 466.4 %all-gather.9.cloned.1.call-start = ((), (), s32[]{:S(2)}) async-start(), calls=%async_computation.6 | async-start | bytes 33423360 | tf_op jit(solution)/shard_map/all_gather | solution.py:8
  92.4 61.4 %copy-start.6 = (bf16[1280,256]{1,0:T(8,128)(2,1)}, bf16[1280,256]{1,0:T(8,128)(2,1)S(1)}, u32[]{:S(2)}) copy-start(bf16[1280,256]{1,0:T(8,128)(2,1)S(1)} %scatter_custom_fusion.1) | copy-start | bytes 1966084
  95.7 58.2 %copy-start.12 = (bf16[1,256,768]{2,1,0:T(8,128)(2,1)S(1)}, bf16[1,256,768]{2,1,0:T(8,128)(2,1)}, u32[]{:S(2)}) copy-start(bf16[1,256,768]{2,1,0:T(8,128)(2,1)} %param.10) | copy-start | bytes 1179652
  95.7 535.4 %all-reduce.3.cloned.1.call-start = ((), (), s32[]{:S(2)}) async-start(), calls=%async_computation.7 | async-start | bytes 7864320 | tf_op jit(solution)/shard_map/psum | solution.py:28
  153.9 4.0 copy-start.10
  157.9 615.6 %reduce-scatter.5.cloned.1.call-start = ((), (), s32[]{:S(2)}) async-start(), calls=%async_computation.5 | async-start | bytes 2162688 | tf_op jit(solution)/shard_map/reduce_scatter | solution.py:101
  635.0 1.5 copy-start.2
  635.0 1.9 copy-start.8
  635.0 2.6 copy-start.4
  635.8 1.9 copy-start.13
  675.8 1.5 copy-start.5
  675.8 1.7 copy-start.7
  675.8 204.1 %reduce-scatter.3.cloned.1.call-start = ((), (), s32[]{:S(2)}) async-start(), calls=%async_computation.3 | async-start | bytes 2162688 | tf_op jit(solution)/shard_map/reduce_scatter | solution.py:88
  677.4 1.6 copy-start.3
  679.0 1.6 copy-start.9
  679.0 1.8 copy-start.11
  679.0 200.8 %copy-start.1 = (bf16[1,768,256]{2,1,0:T(8,128)(2,1)S(1)}, bf16[1,768,256]{2,1,0:T(8,128)(2,1)}, u32[]{:S(2)}) copy-start(bf16[1,768,256]{2,1,0:T(8,128)(2,1)} %param.12) | copy-start | bytes 1179652
Sparse Core Ops, SparseCore 0:
  11.1 62.9 all-gather.4
  77.3 58.2 all-gather.6
  137.6 337.3 all-gather.8
  477.3 153.6 all-reduce.2
  675.9 97.5 reduce-scatter.4
  778.3 101.5 reduce-scatter.2
